TPU v7x, 32 devices: a whole 2x2x4 slice. The times are simulated.
32 devices in a mesh: grp: 4 (over y, x), tok: 8 (over z, core).
Axes of the slice: x: 2, y: 2, z: 4, core: 2. Of those that a mesh axis runs over, the one named last changes fastest.
Arguments:
- queries: bfloat16 [4096, 768], P(('grp', 'tok')), may hold values from -6 to 6
- key_tokens: float32 [4096, 768], P(('grp', 'tok')), may hold values from -6 to 6
- values: float32 [4096, 768], P(('grp', 'tok')), may hold values from -6 to 6
- out_grad: bfloat16 [4096, 768], P(('grp', 'tok')), may hold values from -6 to 6
- w_gate: float32 [768, 768], replicated, may hold values from -0.21875 to 0.21875
- w_up: float32 [768, 768], replicated, may hold values from -0.21875 to 0.21875
- w_down: float32 [768, 768], replicated, may hold values from -0.21875 to 0.21875
Outputs:
- d_queries: bfloat16 [4096, 768], P(('grp', 'tok'))
- d_keys: float32 [4096, 768], P(('grp', 'tok'))
- d_values: float32 [4096, 768], P(('grp', 'tok'))
- d_gate: float32 [768, 768], P('tok')
- d_up: float32 [768, 768], P('tok')
- d_down: float32 [768, 768], P('tok')
All inputs are finite; a program needn't handle non-finite values.
Results may differ from a plain program's by a relative error of at most 0.012.
Values may be sent and summed in bfloat16 or wider, within the bound.
A program may use at most 128 MiB of HBM per device.

v0:
```python
import jax
import jax.numpy as jnp
from jax import lax
from jax.sharding import PartitionSpec as P

STEP_SIZE = 0.02
EPSILON = 1e-06
HIGH = lax.Precision.HIGHEST


def matmul(left, right):
    return jnp.dot(left, right, precision=HIGH, preferred_element_type=jnp.float32)


def key_grad(w_gate, w_up, w_down, key_rows, value_rows):
    hidden_gate = matmul(key_rows, w_gate)
    hidden_up = matmul(key_rows, w_up)
    sig = jax.nn.sigmoid(hidden_gate)
    active = hidden_gate * sig * hidden_up
    error = matmul(active, w_down) - value_rows
    d_active = matmul(error, w_down.T)
    d_hup = d_active * hidden_gate * sig
    d_hgate = d_active * hidden_up * sig * (1.0 + hidden_gate * (1.0 - sig))
    return (matmul(key_rows.T, d_hgate), matmul(key_rows.T, d_hup), matmul(active.T, error))


def query_grad(fast_weights, query_rows, grad_rows):
    fast_gate, fast_up, fast_down = fast_weights
    hidden_gate = jnp.dot(query_rows, fast_gate, preferred_element_type=jnp.float32)
    hidden_up = jnp.dot(query_rows, fast_up, preferred_element_type=jnp.float32)
    sig = jax.nn.sigmoid(hidden_gate)
    active = (hidden_gate * sig * hidden_up).astype(jnp.bfloat16)
    d_active = jnp.dot(grad_rows, fast_down.T, preferred_element_type=jnp.float32)
    d_hup = (d_active * hidden_gate * sig).astype(jnp.bfloat16)
    d_hgate = (d_active * hidden_up * sig * (1.0 + hidden_gate * (1.0 - sig))).astype(jnp.bfloat16)
    d_rows = (
        jnp.dot(d_hgate, fast_gate.T, preferred_element_type=jnp.float32)
        + jnp.dot(d_hup, fast_up.T, preferred_element_type=jnp.float32)
    ).astype(jnp.bfloat16)
    grads = (
        jnp.dot(query_rows.T, d_hgate, preferred_element_type=jnp.float32),
        jnp.dot(query_rows.T, d_hup, preferred_element_type=jnp.float32),
        jnp.dot(active.T, grad_rows, preferred_element_type=jnp.float32),
    )
    return (d_rows, grads)


def column_sums(matrices):
    return tuple((jnp.sum(matrix * matrix, axis=0) for matrix in matrices))


def apply_update(weight_rows, grad_parts, squares, full_width):
    scales = tuple((jnp.sqrt(square / full_width + EPSILON) for square in squares))
    fast_weights = tuple(
        (
            (weight - STEP_SIZE * grad / scale).astype(jnp.bfloat16)
            for weight, grad, scale in zip(weight_rows, grad_parts, scales)
        )
    )
    return (fast_weights, scales)


def back_products(query_parts, grad_parts):
    return tuple(
        (
            jnp.sum(-STEP_SIZE * dpart * gpart, axis=0)
            for dpart, gpart in zip(query_parts, grad_parts)
        )
    )


def normal_back(query_parts, grad_parts, scales, products, full_width):
    return tuple(
        (
            (
                -STEP_SIZE * dpart / scale - gpart * product / (full_width * scale * scale * scale)
            ).astype(jnp.bfloat16)
            for dpart, gpart, scale, product in zip(query_parts, grad_parts, scales, products)
        )
    )


def on_device(queries, key_tokens, values, out_grad, w_gate, w_up, w_down):
    weights = (w_gate, w_up, w_down)
    full_width = w_gate.shape[0]
    tokens_all = key_tokens.shape[0] * lax.axis_size("grp") * lax.axis_size("tok")
    local_grad, pullback = jax.vjp(key_grad, w_gate, w_up, w_down, key_tokens, values)
    row_count = full_width // lax.axis_size("tok")
    row_start = lax.axis_index("tok") * row_count
    grad_parts = (
        lax.psum_scatter(local_grad[0], "tok", scatter_dimension=0, tiled=True),
        lax.psum_scatter(local_grad[1], "tok", scatter_dimension=0, tiled=True),
        lax.psum_scatter(local_grad[2], "tok", scatter_dimension=0, tiled=True),
    )
    grad_parts = lax.psum((grad_parts[0], grad_parts[1], grad_parts[2]), "grp")
    grad_squares = column_sums(grad_parts)
    squares = lax.psum((grad_squares[0], grad_squares[1], grad_squares[2]), "tok")
    weight_rows = tuple(
        (lax.dynamic_slice_in_dim(weight, row_start, row_count, 0) for weight in weights)
    )
    fast_parts, scales = apply_update(weight_rows, grad_parts, squares, full_width)
    fast_weights = (
        lax.all_gather(fast_parts[0], "tok", axis=0, tiled=True),
        lax.all_gather(fast_parts[1], "tok", axis=0, tiled=True),
        lax.all_gather(fast_parts[2], "tok", axis=0, tiled=True),
    )
    d_queries, query_local = query_grad(fast_weights, queries, out_grad)
    query_parts = (
        lax.psum_scatter(query_local[0], "tok", scatter_dimension=0, tiled=True),
        lax.psum_scatter(query_local[1], "tok", scatter_dimension=0, tiled=True),
        lax.psum_scatter(query_local[2], "tok", scatter_dimension=0, tiled=True),
    )
    query_parts = lax.psum((query_parts[0], query_parts[1], query_parts[2]), "grp")
    local_products = back_products(query_parts, grad_parts)
    products = lax.psum((local_products[0], local_products[1], local_products[2]), "tok")
    cot_parts = normal_back(query_parts, grad_parts, scales, products, full_width)
    rounded = (
        lax.all_gather(cot_parts[0], "tok", axis=0, tiled=True),
        lax.all_gather(cot_parts[1], "tok", axis=0, tiled=True),
        lax.all_gather(cot_parts[2], "tok", axis=0, tiled=True),
    )
    cotangent = tuple((item.astype(jnp.float32) for item in rounded))
    second = pullback(cotangent)
    combined = tuple((left + right for left, right in zip(query_local, second[:3])))
    summed = (
        lax.psum_scatter(combined[0], "tok", scatter_dimension=0, tiled=True),
        lax.psum_scatter(combined[1], "tok", scatter_dimension=0, tiled=True),
        lax.psum_scatter(combined[2], "tok", scatter_dimension=0, tiled=True),
    )
    summed = lax.psum((summed[0], summed[1], summed[2]), "grp")
    inverse = 1.0 / tokens_all
    return (
        d_queries,
        second[3],
        second[4],
        summed[0] * inverse,
        summed[1] * inverse,
        summed[2] * inverse,
    )


def solution(mesh):
    placed = (
        P(("grp", "tok"), None),
        P(("grp", "tok"), None),
        P(("grp", "tok"), None),
        P(("grp", "tok"), None),
        P(),
        P(),
        P(),
    )
    return jax.shard_map(
        on_device,
        mesh=mesh,
        in_specs=placed,
        out_specs=(
            P(("grp", "tok"), None),
            P(("grp", "tok"), None),
            P(("grp", "tok"), None),
            P("tok", None),
            P("tok", None),
            P("tok", None),
        ),
        check_vma=False,
    )
```

profile of v0, /device:TPU:0, one launch (start us, length us, event | category | flops | bytes accessed | tf_op | source)
XLA Modules:
  0.0 798.5 jit_solution(9272449964308866308)
XLA Ops:
  8.2 3.2 fusion.25
  11.4 1.5 fusion.18
  13.1 1.4 convolution_subtract_fusion
  14.6 3.4 fusion.24
  18.7 3.5 convolution_bitcast_fusion.3
  22.3 4.6 convolution_bitcast_fusion.2
  27.0 35.2 %reduce-scatter.12.cloned.1.call-done = f32[96,768]{1,0:T(8,128)} async-done(((f32[768,768]{1,0:T(8,128)}), f32[96,768]{1,0:T(8,128)}) %reduce-scatter.12.cloned.1.call-update) | async-done | bytes 294928 | tf_op jit(solution)/shard_map/reduce_scatter | solution.py:92
  62.2 38.3 %reduce-scatter.14.cloned.1.call-done = f32[96,768]{1,0:T(8,128)} async-done(((f32[768,768]{1,0:T(8,128)}), f32[96,768]{1,0:T(8,128)}) %reduce-scatter.14.cloned.1.call-update) | async-done | bytes 294928 | tf_op jit(solution)/shard_map/reduce_scatter | solution.py:91
  100.6 47.9 %all-reduce.17.cloned.1.call-done = (f32[96,768]{1,0:T(8,128)}, f32[96,768]{1,0:T(8,128)}) async-done(((f32[96,768]{1,0:T(8,128)}, f32[96,768]{1,0:T(8,128)}), (f32[96,768]{1,0:T(8,128)}, f32[96,768]{1,0:T(8,128)})) %all-reduce.17.cloned.1.call-update) | async-done | bytes 589840 | tf_op jit(solution)/shard_map/psum | solution.py:95
  150.4 16.1 %all-reduce.1 = (f32[768]{0:T(1024)S(1)}, f32[768]{0:T(1024)S(1)}) all-reduce(f32[768]{0:T(1024)S(1)} %multiply_reduce_fusion.3, f32[768]{0:T(1024)S(1)} %multiply_reduce_fusion.4), channel_id=1, replica_groups=mesh['grp'=4,'tok'=8] {'tok'}, use_global_device_ids=true, to_apply=%region_11.0 | all-reduce | flops 1536 | bytes 12288 | tf_op jit(solution)/shard_map/psum | solution.py:97
  167.1 1.8 subtract_convert_fusion.3
  169.0 1.8 subtract_convert_fusion.4
  171.1 4.5 fusion.26
  175.7 13.4 %all-gather.11.cloned.1.call-done = bf16[768,768]{1,0:T(8,128)(2,1)} async-done(((bf16[96,768]{1,0:T(8,128)(2,1)}), bf16[768,768]{1,0:T(8,128)(2,1)}) %all-gather.11.cloned.1.call-update) | async-done | bytes 1179664 | tf_op jit(solution)/shard_map/all_gather | solution.py:103
  189.1 2.5 convolution_bitcast_fusion.4
  191.5 22.1 %all-gather.9.cloned.1.call-done = bf16[768,768]{1,0:T(8,128)(2,1)} async-done(((bf16[96,768]{1,0:T(8,128)(2,1)}), bf16[768,768]{1,0:T(8,128)(2,1)}) %all-gather.9.cloned.1.call-update) | async-done | bytes 1179664 | tf_op jit(solution)/shard_map/all_gather | solution.py:104
  213.6 1.7 convolution_bitcast_fusion.5
  216.1 3.0 fusion.9
  219.1 33.4 %reduce-scatter.10.cloned.1.call-done = f32[96,768]{1,0:T(8,128)} async-done(((f32[768,768]{1,0:T(8,128)}), f32[96,768]{1,0:T(8,128)}) %reduce-scatter.10.cloned.1.call-update) | async-done | bytes 294928 | tf_op jit(solution)/shard_map/reduce_scatter | solution.py:93
  252.5 38.2 %reduce-scatter.20.cloned.1.call-done = f32[96,768]{1,0:T(8,128)} async-done(((f32[768,768]{1,0:T(8,128)}), f32[96,768]{1,0:T(8,128)}) %reduce-scatter.20.cloned.1.call-update) | async-done | bytes 294928 | tf_op jit(solution)/shard_map/reduce_scatter | solution.py:111
  290.8 47.8 %all-reduce.15.cloned.1.call-done = (f32[96,768]{1,0:T(8,128)}, f32[96,768]{1,0:T(8,128)}) async-done(((f32[96,768]{1,0:T(8,128)}, f32[96,768]{1,0:T(8,128)}), (f32[96,768]{1,0:T(8,128)}, f32[96,768]{1,0:T(8,128)})) %all-reduce.15.cloned.1.call-update) | async-done | bytes 589840 | tf_op jit(solution)/shard_map/psum | solution.py:95
  338.7 1.7 multiply_reduce_fusion
  340.4 16.4 %psum.106 = f32[768]{0:T(1024)} all-reduce(f32[768]{0:T(1024)S(1)} %get-tuple-element.7), channel_id=1, replica_groups=mesh['grp'=4,'tok'=8] {'tok'}, use_global_device_ids=true, to_apply=%region_3.0 | all-reduce | flops 768 | bytes 6144 | tf_op jit(solution)/shard_map/psum | solution.py:97
  356.7 1.3 multiply_multiply_fusion
  358.0 1.7 subtract_convert_fusion.5
  359.8 20.1 %all-gather.7.cloned.1.call-done = bf16[768,768]{1,0:T(8,128)(2,1)} async-done(((bf16[96,768]{1,0:T(8,128)(2,1)}), bf16[768,768]{1,0:T(8,128)(2,1)}) %all-gather.7.cloned.1.call-update) | async-done | bytes 1179664 | tf_op jit(solution)/shard_map/all_gather | solution.py:105
  379.9 2.9 multiply_convert_fusion.1
  383.4 1.9 convolution_bitcast_fusion.1
  385.4 3.0 convolution_bitcast_fusion
  388.5 33.8 %reduce-scatter.16.cloned.1.call-done = f32[96,768]{1,0:T(8,128)} async-done(((f32[768,768]{1,0:T(8,128)}), f32[96,768]{1,0:T(8,128)}) %reduce-scatter.16.cloned.1.call-update) | async-done | bytes 294928 | tf_op jit(solution)/shard_map/reduce_scatter | solution.py:110
  422.2 38.3 %reduce-scatter.18.cloned.1.call-done = f32[96,768]{1,0:T(8,128)} async-done(((f32[768,768]{1,0:T(8,128)}), f32[96,768]{1,0:T(8,128)}) %reduce-scatter.18.cloned.1.call-update) | async-done | bytes 294928 | tf_op jit(solution)/shard_map/reduce_scatter | solution.py:109
  460.6 47.6 %all-reduce.13.cloned.1.call-done = (f32[96,768]{1,0:T(8,128)}, f32[96,768]{1,0:T(8,128)}) async-done(((f32[96,768]{1,0:T(8,128)}, f32[96,768]{1,0:T(8,128)}), (f32[96,768]{1,0:T(8,128)}, f32[96,768]{1,0:T(8,128)})) %all-reduce.13.cloned.1.call-update) | async-done | bytes 589840 | tf_op jit(solution)/shard_map/psum | solution.py:113
  508.3 1.9 multiply_reduce_fusion.1
  510.2 28.0 %all-reduce = (f32[768]{0:T(1024)}, f32[768]{0:T(1024)}, f32[768]{0:T(1024)}) all-reduce(f32[768]{0:T(1024)} %get-tuple-element.42, f32[768]{0:T(1024)} %get-tuple-element.41, f32[768]{0:T(1024)} %get-tuple-element.6), channel_id=1, replica_groups=mesh['grp'=4,'tok'=8] {'tok'}, use_global_device_ids=true, to_apply=%region_15.0 | all-reduce | flops 2304 | bytes 18432 | tf_op jit(solution)/shard_map/psum | solution.py:115
  538.2 1.8 subtract_convert_fusion.1
  540.0 1.8 subtract_convert_fusion.2
  541.9 1.8 subtract_convert_fusion
  543.7 16.4 %all-gather.15.cloned.1.call-done = bf16[768,768]{1,0:T(8,128)(2,1)} async-done(((bf16[96,768]{1,0:T(8,128)(2,1)}), bf16[768,768]{1,0:T(8,128)(2,1)}) %all-gather.15.cloned.1.call-update) | async-done | bytes 1179664 | tf_op jit(solution)/shard_map/all_gather | solution.py:118
  560.1 2.7 convolution_bitcast_fusion.7
  562.8 21.9 %all-gather.13.cloned.1.call-done = bf16[768,768]{1,0:T(8,128)(2,1)} async-done(((bf16[96,768]{1,0:T(8,128)(2,1)}), bf16[768,768]{1,0:T(8,128)(2,1)}) %all-gather.13.cloned.1.call-update) | async-done | bytes 1179664 | tf_op jit(solution)/shard_map/all_gather | solution.py:119
  584.7 2.9 multiply_add_fusion.1
  588.3 2.2 fusion.28
  590.5 18.7 %all-gather.17.cloned.1.call-done = bf16[768,768]{1,0:T(8,128)(2,1)} async-done(((bf16[96,768]{1,0:T(8,128)(2,1)}), bf16[768,768]{1,0:T(8,128)(2,1)}) %all-gather.17.cloned.1.call-update) | async-done | bytes 1179664 | tf_op jit(solution)/shard_map/all_gather | solution.py:120
  609.2 2.8 add_negate_fusion
  612.1 2.5 fusion.1
  614.6 2.3 fusion.7
  617.7 3.5 bitcast_add_fusion
  621.3 1.6 copy-done.3
  622.9 4.5 bitcast_add_fusion.1
  627.7 3.4 fusion.29
  631.1 3.8 add_add_fusion
  636.2 1.6 fusion.27
  637.8 2.3 fusion.3
  640.0 1.3 fusion.21
  641.3 16.8 %reduce-scatter.24.cloned.1.call-done = f32[96,768]{1,0:T(8,128)} async-done(((f32[768,768]{1,0:T(8,128)}), f32[96,768]{1,0:T(8,128)}) %reduce-scatter.24.cloned.1.call-update) | async-done | bytes 294928 | tf_op jit(solution)/shard_map/reduce_scatter | solution.py:127
  658.1 38.1 %reduce-scatter.22.cloned.1.call-done = f32[96,768]{1,0:T(8,128)} async-done(((f32[768,768]{1,0:T(8,128)}), f32[96,768]{1,0:T(8,128)}) %reduce-scatter.22.cloned.1.call-update) | async-done | bytes 294928 | tf_op jit(solution)/shard_map/reduce_scatter | solution.py:126
  696.2 38.0 %reduce-scatter.26.cloned.1.call-done = f32[96,768]{1,0:T(8,128)} async-done(((f32[768,768]{1,0:T(8,128)}), f32[96,768]{1,0:T(8,128)}) %reduce-scatter.26.cloned.1.call-update) | async-done | bytes 294928 | tf_op jit(solution)/shard_map/reduce_scatter | solution.py:128
  734.3 1.3 convolution_add_fusion.4
  735.6 4.4 convolution_add_fusion.2
  740.1 3.3 convolution_add_fusion.1
  743.4 43.3 %all-reduce.11.cloned.1.call-done = (f32[96,768]{1,0:T(8,128)}, f32[96,768]{1,0:T(8,128)}, f32[96,768]{1,0:T(8,128)}) async-done(((f32[96,768]{1,0:T(8,128)}, f32[96,768]{1,0:T(8,128)}, f32[96,768]{1,0:T(8,128)}), (f32[96,768]{1,0:T(8,128)}, f32[96,768]{1,0:T(8,128)}, f32[96,768]{1,0:T(8,128)})) %all-reduce.11.cloned.1.call-update) | async-done | bytes 884752 | tf_op jit(solution)/shard_map/psum | solution.py:130
  786.7 1.7 broadcast_multiply_fusion.2
  788.4 1.7 broadcast_multiply_fusion.1
  790.1 1.7 broadcast_multiply_fusion
  (111 shorter events, 10.4 us)
Async XLA Ops:
  7.2 1.0 copy-start
  7.2 55.0 %reduce-scatter.12.cloned.1.call-start = ((), (), s32[]{:S(2)}) async-start(), calls=%async_computation.11 | async-start | bytes 2654208 | tf_op jit(solution)/shard_map/reduce_scatter | solution.py:92
  8.2 3.2 copy-start.6
  11.4 1.7 copy-start.1
  11.4 1.7 copy-start.34
  12.9 5.1 copy-start.11
  14.6 3.4 copy-start.7
  18.0 0.7 copy-start.21
  22.3 78.2 %reduce-scatter.14.cloned.1.call-start = ((), (), s32[]{:S(2)}) async-start(), calls=%async_computation.13 | async-start | bytes 2654208 | tf_op jit(solution)/shard_map/reduce_scatter | solution.py:91
  26.9 121.5 %all-reduce.17.cloned.1.call-start = ((), (), s32[]{:S(2)}) async-start(), calls=%async_computation.27 | async-start | bytes 1179648 | tf_op jit(solution)/shard_map/psum | solution.py:95
  100.5 88.5 %all-gather.11.cloned.1.call-start = ((), (), s32[]{:S(2)}) async-start(), calls=%async_computation.14 | async-start | bytes 1327104 | tf_op jit(solution)/shard_map/all_gather | solution.py:103
  168.9 44.7 %all-gather.9.cloned.1.call-start = ((), (), s32[]{:S(2)}) async-start(), calls=%async_computation.12 | async-start | bytes 1327104 | tf_op jit(solution)/shard_map/all_gather | solution.py:104
  170.7 81.8 %reduce-scatter.10.cloned.1.call-start = ((), (), s32[]{:S(2)}) async-start(), calls=%async_computation.9 | async-start | bytes 2654208 | tf_op jit(solution)/shard_map/reduce_scatter | solution.py:93
  175.7 115.1 %reduce-scatter.20.cloned.1.call-start = ((), (), s32[]{:S(2)}) async-start(), calls=%async_computation.19 | async-start | bytes 2654208 | tf_op jit(solution)/shard_map/reduce_scatter | solution.py:111
  215.3 0.8 copy-start.28
  219.1 119.6 %all-reduce.15.cloned.1.call-start = ((), (), s32[]{:S(2)}) async-start(), calls=%async_computation.26 | async-start | bytes 1179648 | tf_op jit(solution)/shard_map/psum | solution.py:95
  290.8 89.1 %all-gather.7.cloned.1.call-start = ((), (), s32[]{:S(2)}) async-start(), calls=%async_computation.10 | async-start | bytes 1327104 | tf_op jit(solution)/shard_map/all_gather | solution.py:105
  359.7 62.5 %reduce-scatter.16.cloned.1.call-start = ((), (), s32[]{:S(2)}) async-start(), calls=%async_computation.15 | async-start | bytes 2654208 | tf_op jit(solution)/shard_map/reduce_scatter | solution.py:110
  379.9 3.5 copy-start.27
  382.7 0.7 copy-start.33
  385.4 75.2 %reduce-scatter.18.cloned.1.call-start = ((), (), s32[]{:S(2)}) async-start(), calls=%async_computation.17 | async-start | bytes 2654208 | tf_op jit(solution)/shard_map/reduce_scatter | solution.py:109
  388.4 119.8 %all-reduce.13.cloned.1.call-start = ((), (), s32[]{:S(2)}) async-start(), calls=%async_computation.25 | async-start | bytes 1179648 | tf_op jit(solution)/shard_map/psum | solution.py:113
  460.6 99.6 %all-gather.15.cloned.1.call-start = ((), (), s32[]{:S(2)}) async-start(), calls=%async_computation.18 | async-start | bytes 1327104 | tf_op jit(solution)/shard_map/all_gather | solution.py:118
  540.0 44.7 %all-gather.13.cloned.1.call-start = ((), (), s32[]{:S(2)}) async-start(), calls=%async_computation.16 | async-start | bytes 1327104 | tf_op jit(solution)/shard_map/all_gather | solution.py:119
  541.8 67.4 %all-gather.17.cloned.1.call-start = ((), (), s32[]{:S(2)}) async-start(), calls=%async_computation.20 | async-start | bytes 1327104 | tf_op jit(solution)/shard_map/all_gather | solution.py:120
  543.7 114.5 %reduce-scatter.24.cloned.1.call-start = ((), (), s32[]{:S(2)}) async-start(), calls=%async_computation.22 | async-start | bytes 2654208 | tf_op jit(solution)/shard_map/reduce_scatter | solution.py:127
  587.5 0.8 copy-start.18
  609.2 2.9 copy-start.9
  609.2 5.4 copy-start.30
  612.0 2.6 copy-start.16
  612.0 2.6 copy-start.8
  612.0 2.6 copy-start.12
  612.0 2.6 copy-start.15
  612.0 2.6 copy-start.19
  612.0 2.6 copy-start.22
  612.0 2.6 copy-start.24
  612.0 2.6 copy-start.29
  614.6 3.1 copy-start.4
  617.0 0.8 copy-start.26
  621.3 1.7 copy-start.3
  621.3 74.9 %reduce-scatter.22.cloned.1.call-start = ((), (), s32[]{:S(2)}) async-start(), calls=%async_computation.21 | async-start | bytes 2654208 | tf_op jit(solution)/shard_map/reduce_scatter | solution.py:126
  627.4 3.7 copy-start.2
  627.5 106.8 %reduce-scatter.26.cloned.1.call-start = ((), (), s32[]{:S(2)}) async-start(), calls=%async_computation.23 | async-start | bytes 2654208 | tf_op jit(solution)/shard_map/reduce_scatter | solution.py:128
  627.7 3.4 copy-start.10
  627.7 3.4 copy-start.17
  634.9 1.3 copy-start.13
  634.9 2.9 copy-start.14
  634.9 151.8 %all-reduce.11.cloned.1.call-start = ((), (), s32[]{:S(2)}) async-start(), calls=%async_computation.24 | async-start | bytes 1769472 | tf_op jit(solution)/shard_map/psum | solution.py:130
  636.2 3.9 copy-start.23
  636.2 3.9 copy-start.31
  637.8 96.5 %copy-start.20 = (f32[128,768]{1,0:T(8,128)S(1)}, f32[128,768]{1,0:T(8,128)}, u32[]{:S(2)}) copy-start(f32[128,768]{1,0:T(8,128)} %get-tuple-element.27) | copy-start | bytes 1179652
  637.8 96.5 %copy-start.32 = (bf16[768,768]{1,0:T(8,128)(2,1)S(1)}, bf16[768,768]{1,0:T(8,128)(2,1)}, u32[]{:S(2)}) copy-start(bf16[768,768]{1,0:T(8,128)(2,1)} %all-gather.15.cloned.1.call-done) | copy-start | bytes 3538948
  735.6 4.5 copy-start.5
  735.6 4.5 copy-start.25
Sparse Core Ops, SparseCore 0:
  22.4 39.7 reduce-scatter.11
  64.5 35.9 reduce-scatter.13
  103.5 44.8 all-reduce.16
  169.0 19.9 all-gather.10
  191.1 22.4 all-gather.8
  215.7 36.7 reduce-scatter.9
  254.8 35.8 reduce-scatter.19
  293.7 44.8 all-reduce.14
  359.8 19.9 all-gather.6
  385.5 36.6 reduce-scatter.15
  424.5 35.9 reduce-scatter.17
  463.4 44.8 all-reduce.12
  540.1 19.9 all-gather.14
  562.2 22.4 all-gather.12
  586.7 22.4 all-gather.16
  621.4 36.6 reduce-scatter.23
  660.3 35.8 reduce-scatter.21
  698.4 35.8 reduce-scatter.25
  737.6 49.0 all-reduce.10
where the time goes:
time: 808 us; the launch traced here: 799 us
  waiting for transfers between devices  610 us (75%)
  matrix products  81.6 us (10%)
  blocking collectives  60.5 us (7%)
  other arithmetic  23.1 us (3%)
  between operations  14.6 us (2%)
    psum x2, waiting for transfers between devices, on_device(): grad_parts = lax.psum((grad_parts[0], grad_parts[1], grad_parts[2]), 'grp')  95.7 us
    dot_general x21, matrix products, matmul(): jnp.dot(left, right, precision=HIGH, preferred_element_type=jnp.float32)  62.9 us
    psum x1, waiting for transfers between devices, on_device(): lax.psum((query_parts[0], query_parts[1], query_parts[2]), 'grp')  47.6 us
    psum x1, waiting for transfers between devices, on_device(): summed = lax.psum((summed[0], summed[1], summed[2]), 'grp')  43.3 us
    reduce_scatter x1, waiting for transfers between devices, on_device(): lax.psum_scatter(query_local[0], 'tok', scatter_dimension=0, tiled=True)  38.3 us
    reduce_scatter x1, waiting for transfers between devices, on_device(): lax.psum_scatter(local_grad[0], 'tok', scatter_dimension=0, tiled=True)  38.3 us
    reduce_scatter x1, waiting for transfers between devices, on_device(): lax.psum_scatter(query_local[2], 'tok', scatter_dimension=0, tiled=True)  38.2 us
    reduce_scatter x1, waiting for transfers between devices, on_device(): lax.psum_scatter(combined[0], 'tok', scatter_dimension=0, tiled=True)  38.1 us
  transfers between devices with their start and end apart: 19, of which 19 were waited for; matrix products, arithmetic and copies ran while one was open for 7% of the time, Pallas kernels for 0%

commit v1 on v0

v1 whole, which is shorter than its diff:
```python
import functools

import jax
import jax.numpy as jnp
from jax import lax
from jax.experimental import pallas as pl
from jax.experimental.pallas import tpu as pltpu
from jax.sharding import PartitionSpec as P

STEP_SIZE = 0.02
EPSILON = 1e-06
MESH = pl.DeviceIdType.MESH
BF = jnp.bfloat16
F32 = jnp.float32


def matmul(left, right):
    return jnp.dot(left.astype(BF), right.astype(BF), preferred_element_type=F32)


def key_grad(w_gate, w_up, w_down, key_rows, value_rows):
    hidden_gate = matmul(key_rows, w_gate)
    hidden_up = matmul(key_rows, w_up)
    sig = jax.nn.sigmoid(hidden_gate)
    active = hidden_gate * sig * hidden_up
    error = matmul(active, w_down) - value_rows
    d_active = matmul(error, w_down.T)
    d_hup = d_active * hidden_gate * sig
    d_hgate = d_active * hidden_up * sig * (1.0 + hidden_gate * (1.0 - sig))
    return (matmul(d_hgate.T, key_rows), matmul(d_hup.T, key_rows), matmul(error.T, active))


def query_grad(fast_t, query_rows, grad_rows):
    gate_t, up_t, down_t = fast_t
    hidden_gate = jnp.dot(query_rows, gate_t.T, preferred_element_type=F32)
    hidden_up = jnp.dot(query_rows, up_t.T, preferred_element_type=F32)
    sig = jax.nn.sigmoid(hidden_gate)
    active = (hidden_gate * sig * hidden_up).astype(BF)
    d_active = jnp.dot(grad_rows, down_t, preferred_element_type=F32)
    d_hup = (d_active * hidden_gate * sig).astype(BF)
    d_hgate = (d_active * hidden_up * sig * (1.0 + hidden_gate * (1.0 - sig))).astype(BF)
    d_rows = (
        jnp.dot(d_hgate, gate_t, preferred_element_type=F32)
        + jnp.dot(d_hup, up_t, preferred_element_type=F32)
    ).astype(BF)
    return (d_rows, active, d_hgate, d_hup)


def position(zs, gs):
    g = lax.axis_index("grp")
    t = lax.axis_index("tok")
    return g, t // 2, lax.rem(t, 2)


def greet(zs, gs, g, z, core):
    barrier = pltpu.get_barrier_semaphore()
    pl.semaphore_signal(barrier, inc=1, device_id=(g, 2 * z + 1 - core), device_id_type=MESH)
    for d in range(1, zs):
        peer = (g, 2 * lax.rem(z + d, zs) + core)
        pl.semaphore_signal(barrier, inc=1, device_id=peer, device_id_type=MESH)
    for d in range(1, gs):
        peer = (lax.rem(g + d, gs), 2 * z + core)
        pl.semaphore_signal(barrier, inc=1, device_id=peer, device_id_type=MESH)
    pl.semaphore_wait(barrier, zs + gs - 1)


def remote(src, dst, send, recv, peer):
    return pltpu.make_async_remote_copy(
        src_ref=src, dst_ref=dst, send_sem=send, recv_sem=recv,
        device_id=peer, device_id_type=MESH,
    )


def reduce_body(zs, gs, x, out, rc, s1, ra1, rb1, sa, sb, ra2, rb2,
                cs, cr, a1s, a1r, b1s, b1r, a2s, a2r, b2s, b2r):
    g, z, core = position(zs, gs)
    width = x.shape[-1]
    half = width // 2
    left, right = pl.ds(0, half), pl.ds(half, half)
    greet(zs, gs, g, z, core)
    twin = (g, 2 * z + 1 - core)
    pending = []
    pair = []
    order = list(range(1, zs)) + [0]
    for d in order:
        zc = lax.rem(z + d, zs)
        copy = remote(x.at[zc, 1 - core], rc.at[d], cs.at[d], cr.at[d], twin)
        copy.start()
        pair.append((d, zc, copy))
    first_a, first_b = [], []
    for d, zc, copy in pair:
        copy.wait_recv()
        for k in range(gs):
            s1[zc, k] = (x[zc, core, k].astype(F32) + rc[d, k].astype(F32)).astype(BF)
        if d:
            c = remote(s1.at[zc, :, :, left], ra1.at[d - 1], a1s.at[d - 1], a1r.at[d - 1],
                       (g, 2 * zc + core))
            c.start()
            first_a.append(c)
        for e in range(1, gs):
            gc = lax.rem(g + e, gs)
            c = remote(s1.at[zc, gc, :, right], rb1.at[e - 1, zc], b1s.at[e - 1, d],
                       b1r.at[e - 1, d], (gc, 2 * z + core))
            c.start()
            first_b.append((d, c))
    second = []
    for d in order:
        zc = lax.rem(z + d, zs)
        for dd, c in first_b:
            if dd == d:
                c.wait_recv()
        total = s1[zc, g, :, half:].astype(F32)
        for e in range(1, gs):
            total = total + rb1[e - 1, zc].astype(F32)
        if d:
            sb[d - 1] = total.astype(BF)
            c = remote(sb.at[d - 1], rb2.at[d - 1], b2s.at[d - 1], b2r.at[d - 1],
                       (g, 2 * zc + core))
            c.start()
            second.append(c)
        else:
            out[:, half:] = total
    for c in first_a:
        c.wait_recv()
    for e in list(range(1, gs)) + [0]:
        gc = lax.rem(g + e, gs)
        total = s1[z, gc, :, :half].astype(F32)
        for d in range(1, zs):
            total = total + ra1[d - 1, gc].astype(F32)
        if e:
            sa[e - 1] = total.astype(BF)
            c = remote(sa.at[e - 1], ra2.at[e - 1], a2s.at[e - 1], a2r.at[e - 1],
                       (gc, 2 * z + core))
            c.start()
            second.append(c)
        else:
            out[:, :half] = total
    for c in second:
        c.wait_recv()
    total = out[:, half:]
    for d in range(1, zs):
        total = total + rb2[d - 1].astype(F32)
    out[:, half:] = total
    total = out[:, :half]
    for e in range(1, gs):
        total = total + ra2[e - 1].astype(F32)
    out[:, :half] = total
    for d, zc, c in pair:
        c.wait_send()
    for c in first_a:
        c.wait_send()
    for d, c in first_b:
        c.wait_send()
    for c in second:
        c.wait_send()


VM = pltpu.VMEM
DMA = pltpu.SemaphoreType.DMA


def reduce_all(x, number):
    zs, _, gs, rows, width = x.shape
    half = width // 2
    return pl.pallas_call(
        functools.partial(reduce_body, zs, gs),
        out_shape=jax.ShapeDtypeStruct((rows, width), F32),
        in_specs=[pl.BlockSpec(memory_space=pltpu.VMEM)],
        out_specs=pl.BlockSpec(memory_space=pltpu.VMEM),
        scratch_shapes=[
            VM((zs, gs, rows, width), BF),
            VM((zs, gs, rows, width), BF),
            VM((zs - 1, gs, rows, half), BF),
            VM((gs - 1, zs, rows, half), BF),
            VM((gs - 1, rows, half), BF),
            VM((zs - 1, rows, half), BF),
            VM((gs - 1, rows, half), BF),
            VM((zs - 1, rows, half), BF),
            DMA((zs,)), DMA((zs,)),
            DMA((zs - 1,)), DMA((zs - 1,)),
            DMA((gs - 1, zs)), DMA((gs - 1, zs)),
            DMA((gs - 1,)), DMA((gs - 1,)),
            DMA((zs - 1,)), DMA((zs - 1,)),
        ],
        compiler_params=pltpu.CompilerParams(collective_id=number, has_side_effects=True),
    )(x)


def gather_body(zs, gs, y, out, cs, cr, a1s, a1r, b1s, b1r, a2s, a2r, b2s, b2r, ls):
    g, z, core = position(zs, gs)
    width = y.shape[-1]
    half = width // 2
    left, right = pl.ds(0, half), pl.ds(half, half)
    greet(zs, gs, g, z, core)
    twin = (g, 2 * z + 1 - core)
    own = pltpu.make_async_copy(y, out.at[z, core, g], ls)
    own.start()
    to_g = lambda e: (lax.rem(g + e, gs), 2 * z + core)
    to_z = lambda d: (g, 2 * lax.rem(z + d, zs) + core)
    first_a, first_b = [], []
    for e in range(1, gs):
        c = remote(y.at[:, left], out.at[z, core, g, :, left], a1s.at[e - 1], a1r.at[e - 1], to_g(e))
        c.start()
        first_a.append(c)
    for d in range(1, zs):
        c = remote(y.at[:, right], out.at[z, core, g, :, right], b1s.at[d - 1], b1r.at[d - 1], to_z(d))
        c.start()
        first_b.append(c)
    own.wait()
    sent = []
    second_a, second_b = [], []

    def hand(src, slot):
        c = remote(src, src, cs.at[slot], cr.at[slot], twin)
        c.start()
        sent.append(c)

    for c in first_a:
        c.wait_recv()
    for d in range(1, zs):
        part = out.at[z, core, :, :, left]
        c = remote(part, part, a2s.at[d - 1], a2r.at[d - 1], to_z(d))
        c.start()
        second_a.append(c)
    for c in first_b:
        c.wait_recv()
    for e in range(1, gs):
        part = out.at[:, core, g, :, right]
        c = remote(part, part, b2s.at[e - 1], b2r.at[e - 1], to_g(e))
        c.start()
        second_b.append(c)
    hand(out.at[z, core, :, :, left], 0)
    hand(out.at[:, core, g, :, right], 1)
    slot = 2
    for d in range(1, zs):
        second_a[d - 1].wait_recv()
        hand(out.at[lax.rem(z - d + zs, zs), core, :, :, left], slot)
        slot += 1
    for e in range(1, gs):
        second_b[e - 1].wait_recv()
        hand(out.at[:, core, lax.rem(g - e + gs, gs), :, right], slot)
        slot += 1
    for c in sent:
        c.wait()
    for c in first_a + first_b + second_a + second_b:
        c.wait_send()


def gather_all(y, zs, gs, number):
    rows, width = y.shape
    return pl.pallas_call(
        functools.partial(gather_body, zs, gs),
        out_shape=jax.ShapeDtypeStruct((zs, 2, gs, rows, width), BF),
        in_specs=[pl.BlockSpec(memory_space=pltpu.VMEM)],
        out_specs=pl.BlockSpec(memory_space=pltpu.VMEM),
        scratch_shapes=[
            DMA((zs + gs,)), DMA((zs + gs,)),
            DMA((gs - 1,)), DMA((gs - 1,)),
            DMA((zs - 1,)), DMA((zs - 1,)),
            DMA((zs - 1,)), DMA((zs - 1,)),
            DMA((gs - 1,)), DMA((gs - 1,)),
            DMA,
        ],
        compiler_params=pltpu.CompilerParams(collective_id=number, has_side_effects=True),
    )(y)


def on_device(queries, key_tokens, values, out_grad, w_gate, w_up, w_down):
    gs, toks = lax.axis_size("grp"), lax.axis_size("tok")
    zs, devices = toks // 2, gs * toks
    full_width = w_gate.shape[0]
    tokens_all = key_tokens.shape[0] * devices
    weights = (w_gate, w_up, w_down)
    rows = 3 * full_width // devices
    direct = 3 * full_width % (8 * devices) == 0 and toks % 4 == 0 and full_width % 256 == 0
    me = lax.axis_index("tok") * gs + lax.axis_index("grp")

    def reduce_units(x, number):
        if direct:
            return reduce_all(x.astype(BF).reshape(zs, 2, gs, rows, full_width), number)
        y = x.reshape(toks, gs * rows, full_width)
        y = lax.psum_scatter(y, "tok", scatter_dimension=0, tiled=True)[0]
        return lax.psum_scatter(y.reshape(gs, rows, full_width), "grp", scatter_dimension=0, tiled=True)[0]

    def gather_units(y, number):
        if direct:
            full = gather_all(y, zs, gs, number)
        else:
            full = lax.all_gather(lax.all_gather(y, "grp"), "tok")
        full = full.reshape(3, full_width, full_width)
        return full[0], full[1], full[2]

    local_grad, pullback = jax.vjp(key_grad, w_gate, w_up, w_down, key_tokens, values)
    grad = reduce_units(jnp.stack(local_grad), 0)
    scale = jnp.sqrt(jnp.sum(grad * grad, axis=1, keepdims=True) / full_width + EPSILON)
    mine = lax.dynamic_slice_in_dim(jnp.concatenate(weights, axis=1), me * rows, rows, 1).T
    fast = (mine - STEP_SIZE * grad / scale).astype(BF)
    fast_t = gather_units(fast, 1)
    d_queries, active, d_hgate, d_hup = query_grad(fast_t, queries, out_grad)
    dot = functools.partial(jnp.dot, preferred_element_type=F32)
    query_local = jnp.stack((dot(d_hgate.T, queries), dot(d_hup.T, queries), dot(out_grad.T, active)))
    query_part = reduce_units(query_local, 2)
    product = jnp.sum(-STEP_SIZE * query_part * grad, axis=1, keepdims=True)
    cot = (
        -STEP_SIZE * query_part / scale - grad * product / (full_width * scale * scale * scale)
    ).astype(BF)
    cotangent = tuple(item.astype(F32) for item in gather_units(cot, 3))
    second = pullback(cotangent)
    plain = (dot(queries.T, d_hgate), dot(queries.T, d_hup), dot(active.T, out_grad))
    combined = jnp.stack(tuple((left + right for left, right in zip(plain, second[:3]))))
    combined = combined.reshape(3, toks, full_width // toks, full_width).transpose(1, 0, 2, 3)
    summed = reduce_units(combined, 4) * (1.0 / tokens_all)
    summed = lax.all_gather(summed.astype(BF), "grp").astype(F32)
    summed = summed.reshape(3, full_width // toks, full_width)
    return (d_queries, second[3], second[4], summed[0], summed[1], summed[2])


def solution(mesh):
    token = P(("grp", "tok"), None)
    return jax.shard_map(
        on_device,
        mesh=mesh,
        in_specs=(token, token, token, token, P(), P(), P()),
        out_specs=(token, token, token, P("tok", None), P("tok", None), P("tok", None)),
        check_vma=False,
    )
```

time: 808 us -> 247 us (0.31); the launches traced: 799 us -> 246 us
  waiting for transfers between devices: 610 us -> 0 us
  Pallas kernels: 0 us -> 170 us
  matrix products: 81.6 us -> 29.3 us
  blocking collectives: 60.5 us -> 9.15 us
  local copies, waits for them, and re-layouts: 7.78 us -> 23.9 us
  between operations: 14.6 us -> 1.14 us
  other arithmetic: 23.1 us -> 12.5 us
    reduce_scatter x9 -> x0, waiting for transfers between devices: 310 us -> none  [the longest x1 38.3 us: on_device(): lax.psum_scatter(query_local[0], 'tok', scatter_dimension=0, tiled=True)]
    psum x4 -> x0, waiting for transfers between devices: 187 us -> none  [the longest x2 95.7 us: on_device(): grad_parts = lax.psum((grad_parts[0], grad_parts[1], grad_parts[2]), 'grp')]
    pallas_call x0 -> x5, Pallas kernels: none -> 170 us  [the longest x3 109 us: reduce_all(): pl.pallas_call(functools.partial(reduce_body, zs, gs), out_shape=jax.Shap...]
    all_gather x6 -> x0, waiting for transfers between devices: 113 us -> none  [the longest x1 22.1 us: on_device(): lax.all_gather(fast_parts[1], 'tok', axis=0, tiled=True)]
    psum x3 -> x0, blocking collectives: 60.5 us -> none  [the longest x2 32.5 us: on_device(): lax.psum((grad_squares[0], grad_squares[1], grad_squares[2]), 'tok')]
    dot_general x29, matrix products: 81.6 us -> 29.3 us  [the longest x21 21.4 us: matmul(): jnp.dot(left.astype(BF), right.astype(BF), preferred_element_type=F32)]
    all_gather x0 -> x1, blocking collectives: none -> 9.15 us  [on_device(): summed = lax.all_gather(summed.astype(BF), 'grp').astype(F32)]
  transfers between devices with their start and end apart: 19 -> 0, of which waited for: 19 -> 0; matrix products, arithmetic and copies ran while one was open for 7% -> 0% of each run, Pallas kernels for 0% -> 0%
where the time goes in v1:
time: 247 us; the launch traced here: 246 us
  Pallas kernels  170 us (69%)
  matrix products  29.3 us (12%)
  local copies, waits for them, and re-layouts  23.9 us (10%)
  other arithmetic  12.5 us (5%)
  blocking collectives  9.15 us (4%)
    pallas_call x3, Pallas kernels, reduce_all(): pl.pallas_call(functools.partial(reduce_body, zs, gs), out_shape=jax.Shap...  109 us
    pallas_call x2, Pallas kernels, gather_all(): pl.pallas_call(functools.partial(gather_body, zs, gs), out_shape=jax.Shap...  60.6 us
    dot_general x21, matrix products, matmul(): jnp.dot(left.astype(BF), right.astype(BF), preferred_element_type=F32)  21.4 us
    unnamed x73, local copies, waits for them, and re-layouts  14.7 us
    all_gather x1, blocking collectives, on_device(): summed = lax.all_gather(summed.astype(BF), 'grp').astype(F32)  9.15 us

profile of v1, /device:TPU:0, one launch (start us, length us, event | category | flops | bytes accessed | tf_op | source)
XLA Modules:
  0.0 245.7 jit_solution(11355242020366915202)
XLA Ops:
  0.7 1.2 convert_element_type.175
  1.8 2.0 fusion.29
  3.9 0.3 multiply_convert_fusion.3
  4.2 1.6 copy-done.12
  5.8 0.1 convert_element_type.179
  6.0 0.3 fusion.5
  6.3 1.3 fusion.42
  7.7 0.5 fusion
  8.1 0.2 copy-done.21
  8.3 0.5 fusion.1
  8.8 0.5 fusion.2
  9.3 2.1 pad_maximum_fusion
  11.5 35.2 %shard_map.118 = f32[72,768]{1,0:T(8,128)} custom-call(bf16[4,2,4,72,768]{4,3,2,1,0:T(8,128)(2,1)} %bitcast.151), custom_call_target="tpu_custom_call" | custom-call | tf_op jit(solution)/shard_map/pallas_call | solution.py:165
  46.7 1.1 multiply_reduce_fusion.1
  47.7 3.1 %copy.29 = f32[768,768]{0,1:T(8,128)} copy(f32[768,768]{1,0:T(8,128)} %param.13) | data formatting | bytes 4718592 | tf_op args[6]
  50.8 3.1 %copy.27 = f32[768,768]{0,1:T(8,128)} copy(f32[768,768]{1,0:T(8,128)} %param.11) | data formatting | bytes 4718592 | tf_op args[4]
  53.9 2.0 copy.28
  55.9 1.7 fusion.48.y
  57.6 30.9 %shard_map.119 = bf16[4,2,4,72,768]{4,3,2,1,0:T(8,128)(2,1)} custom-call(bf16[72,768]{1,0:T(8,128)(2,1)} %fusion.48.y), custom_call_target="tpu_custom_call" | custom-call | tf_op jit(solution)/shard_map/pallas_call | solution.py:251
  88.5 2.0 convolution_bitcast_fusion.1
  90.4 1.8 convolution_bitcast_fusion.2
  92.2 0.4 multiply_convert_fusion.1
  92.7 0.3 fusion.24
  93.0 1.0 fusion.6
  94.0 0.5 fusion.49
  94.5 1.5 copy.33
  96.1 1.5 fusion.57
  97.6 0.5 fusion.56
  98.1 0.2 convert_bitcast_fusion.1
  98.3 0.7 copy-done.4
  99.0 0.7 copy-done.2
  99.8 0.5 copy-done.14
  100.2 1.9 pad_maximum_fusion.1
  102.2 36.6 %shard_map.120 = f32[72,768]{1,0:T(8,128)} custom-call(bf16[4,2,4,72,768]{4,3,2,1,0:T(8,128)(2,1)} %bitcast.152), custom_call_target="tpu_custom_call" | custom-call | tf_op jit(solution)/shard_map/pallas_call | solution.py:165
  138.7 1.1 multiply_reduce_fusion
  139.8 1.7 subtract_convert_fusion.y
  141.5 29.8 %shard_map.121 = bf16[4,2,4,72,768]{4,3,2,1,0:T(8,128)(2,1)} custom-call(bf16[72,768]{1,0:T(8,128)(2,1)} %subtract_convert_fusion.y), custom_call_target="tpu_custom_call" | custom-call | tf_op jit(solution)/shard_map/pallas_call | solution.py:251
  171.3 1.8 fusion.23
  173.2 2.4 fusion.22
  175.6 0.5 fusion.20
  176.1 0.5 fusion.17
  176.6 0.3 fusion.18
  177.0 0.6 multiply_add_fusion.1
  177.6 0.7 copy-done.10
  178.3 1.1 fusion.55
  179.4 0.8 fusion.35
  180.2 0.9 copy-done.5
  181.1 1.6 fusion.4
  182.7 1.5 fusion.3
  184.2 2.4 copy.37
  186.5 2.4 copy.39
  188.9 2.5 %fusion.10 = f32[128,768]{1,0:T(8,128)S(1)} fusion(f32[128,768]{1,0:T(8,128)} %fusion.22, bf16[128,768]{1,0:T(8,128)(2,1)} %copy-done.26, f32[768,768]{1,0:T(8,128)} %param.12), kind=kOutput, calls=%fused_computation.42 | convolution fusion | flops 151781376 | bytes 3342336 | tf_op jit(solution)/shard_map/transpose(jvp())/dot_general | solution.py:18
  191.4 0.1 copy-done.7
  191.5 1.3 fusion.8
  192.8 0.5 fusion.58
  193.3 0.5 add_convert_fusion
  193.8 0.7 copy-done.15
  194.5 0.4 copy-done.16
  194.9 0.4 maximum_bitcast_fusion
  195.3 2.0 copy.40
  197.3 37.3 %shard_map.122 = f32[72,768]{1,0:T(8,128)} custom-call(bf16[4,2,4,72,768]{4,3,2,1,0:T(8,128)(2,1)} %bitcast.153), custom_call_target="tpu_custom_call" | custom-call | tf_op jit(solution)/shard_map/pallas_call | solution.py:165
  234.6 1.0 multiply_convert_fusion.4
  235.6 9.2 %all-gather = bf16[288,768]{1,0:T(8,128)(2,1)S(1)} all-gather(bf16[72,768]{1,0:T(8,128)(2,1)S(1)} %multiply_convert_fusion.4), channel_id=2, replica_groups=mesh['grp'=4,'tok'=8] {'grp'}, dimensions={0}, use_global_device_ids=true | all-gather | bytes 552960 | tf_op jit(solution)/shard_map/all_gather | solution.py:313
  244.7 0.9 fusion.54
  (61 shorter events, 0.2 us)
Async XLA Ops:
  0.6 87.8 %copy-start = (bf16[128,768]{1,0:T(8,128)(2,1)S(1)}, bf16[128,768]{1,0:T(8,128)(2,1)}, u32[]{:S(2)}) copy-start(bf16[128,768]{1,0:T(8,128)(2,1)} %param.7) | copy-start | bytes 589828
  0.6 3.2 %copy-start.6 = (f32[768,768]{1,0:T(8,128)S(1)}, f32[768,768]{1,0:T(8,128)}, u32[]{:S(2)}) copy-start(f32[768,768]{1,0:T(8,128)} %param.12) | copy-start | bytes 7077892
  3.8 2.4 copy-start.17
  3.9 2.0 copy-start.12
  4.2 2.1 copy-start.30
  4.2 1.7 copy-start.32
  5.9 1.7 copy-start.9
  7.6 0.7 copy-start.21
  7.6 1.7 copy-start.19
  53.9 2.0 copy-start.13
  88.4 3.8 %copy-start.11 = (bf16[4,2,4,72,768]{4,3,2,1,0:T(8,128)(2,1)S(1)}, bf16[4,2,4,72,768]{4,3,2,1,0:T(8,128)(2,1)}, u32[]{:S(2)}) copy-start(bf16[4,2,4,72,768]{4,3,2,1,0:T(8,128)(2,1)} %shard_map.119) | copy-start | bytes 10616836
  88.4 3.8 %copy-start.33 = (bf16[128,768]{1,0:T(8,128)(2,1)S(1)}, bf16[128,768]{1,0:T(8,128)(2,1)}, u32[]{:S(2)}) copy-start(bf16[128,768]{1,0:T(8,128)(2,1)} %param.10) | copy-start | bytes 589828
  92.6 1.4 copy-start.27
  92.7 1.4 copy-start.29
  96.1 1.5 copy-start.28
  97.6 1.5 copy-start.4
  98.1 1.7 copy-start.2
  98.1 2.1 copy-start.14
  141.5 31.6 %copy-start.20 = (bf16[768,128]{0,1:T(8,128)(2,1)S(1)}, bf16[768,128]{0,1:T(8,128)(2,1)}, u32[]{:S(2)}) copy-start(bf16[768,128]{0,1:T(8,128)(2,1)} %copy-done.19) | copy-start | bytes 589828
  171.3 4.3 %copy-start.8 = (bf16[4,2,4,72,768]{4,3,2,1,0:T(8,128)(2,1)S(1)}, bf16[4,2,4,72,768]{4,3,2,1,0:T(8,128)(2,1)}, u32[]{:S(2)}) copy-start(bf16[4,2,4,72,768]{4,3,2,1,0:T(8,128)(2,1)} %shard_map.121) | copy-start | bytes 10616836
  175.6 1.4 copy-start.18
  175.6 1.4 copy-start.31
  177.0 1.3 copy-start.10
  177.0 2.3 copy-start.34
  179.4 0.8 copy-start.22
  179.4 1.7 copy-start.5
  180.2 2.5 %copy-start.26 = (bf16[128,768]{1,0:T(8,128)(2,1)}, bf16[128,768]{1,0:T(8,128)(2,1)S(1)}, u32[]{:S(2)}) copy-start(bf16[128,768]{1,0:T(8,128)(2,1)S(1)} %get-tuple-element.7) | copy-start | bytes 589828
  180.2 2.5 %copy-start.24 = (bf16[128,768]{1,0:T(8,128)(2,1)}, bf16[128,768]{1,0:T(8,128)(2,1)S(1)}, u32[]{:S(2)}) copy-start(bf16[128,768]{1,0:T(8,128)(2,1)S(1)} %get-tuple-element.6) | copy-start | bytes 589828
  180.2 2.5 %copy-start.3 = (f32[768,768]{1,0:T(8,128)S(1)}, f32[768,768]{1,0:T(8,128)}, u32[]{:S(2)}) copy-start(f32[768,768]{1,0:T(8,128)} %copy-done.2) | copy-start | bytes 7077892
  188.9 2.6 %copy-start.7 = (f32[768,768]{1,0:T(8,128)S(1)}, f32[768,768]{1,0:T(8,128)}, u32[]{:S(2)}) copy-start(f32[768,768]{1,0:T(8,128)} %param.11) | copy-start | bytes 7077892
  188.9 2.6 %copy-start.25 = (bf16[128,768]{1,0:T(8,128)(2,1)S(1)}, bf16[128,768]{1,0:T(8,128)(2,1)}, u32[]{:S(2)}) copy-start(bf16[128,768]{1,0:T(8,128)(2,1)} %copy-done.24) | copy-start | bytes 589828
  191.5 1.3 copy-start.23
  193.3 1.3 copy-start.15
  193.3 1.6 copy-start.16
  197.3 48.4 %copy-start.1 = (bf16[128,768]{1,0:T(8,128)(2,1)S(1)}, bf16[128,768]{1,0:T(8,128)(2,1)}, u32[]{:S(2)}) copy-start(bf16[128,768]{1,0:T(8,128)(2,1)} %param.7) | copy-start | bytes 589828

commit v2 on v1

--- a/solution.py
+++ b/solution.py
@@ -46,6 +46,10 @@
     return (d_rows, active, d_hgate, d_hup)
 
 
+def cut_of(width):
+    return 128 * (width // 384)
+
+
 def position(zs, gs):
     g = lax.axis_index("grp")
     t = lax.axis_index("tok")
@@ -75,8 +79,8 @@
                 cs, cr, a1s, a1r, b1s, b1r, a2s, a2r, b2s, b2r):
     g, z, core = position(zs, gs)
     width = x.shape[-1]
-    half = width // 2
-    left, right = pl.ds(0, half), pl.ds(half, half)
+    half = cut_of(width)
+    left, right = pl.ds(0, half), pl.ds(half, width - half)
     greet(zs, gs, g, z, core)
     twin = (g, 2 * z + 1 - core)
     pending = []
@@ -159,29 +163,51 @@
 DMA = pltpu.SemaphoreType.DMA
 
 
-def reduce_all(x, number):
+def reduce_gather_body(zs, gs, x, full, part, fs, fr, *scratch):
+    reduce_body(zs, gs, x, part, *scratch)
+    g, z, core = position(zs, gs)
+    full[g] = part[...].astype(BF)
+    copies = []
+    for e in range(1, gs):
+        peer = (lax.rem(g + e, gs), 2 * z + core)
+        c = remote(full.at[g], full.at[g], fs.at[e - 1], fr.at[e - 1], peer)
+        c.start()
+        copies.append(c)
+    for c in copies:
+        c.wait()
+
+
+def reduce_all(x, number, gathered=False):
     zs, _, gs, rows, width = x.shape
-    half = width // 2
+    left = cut_of(width)
+    right = width - left
+    scratch = [
+        VM((zs, gs, rows, width), BF),
+        VM((zs, gs, rows, width), BF),
+        VM((zs - 1, gs, rows, left), BF),
+        VM((gs - 1, zs, rows, right), BF),
+        VM((gs - 1, rows, left), BF),
+        VM((zs - 1, rows, right), BF),
+        VM((gs - 1, rows, left), BF),
+        VM((zs - 1, rows, right), BF),
+        DMA((zs,)), DMA((zs,)),
+        DMA((zs - 1,)), DMA((zs - 1,)),
+        DMA((gs - 1, zs)), DMA((gs - 1, zs)),
+        DMA((gs - 1,)), DMA((gs - 1,)),
+        DMA((zs - 1,)), DMA((zs - 1,)),
+    ]
+    shape = jax.ShapeDtypeStruct((rows, width), F32)
+    body = reduce_body
+    if gathered:
+        shape = jax.ShapeDtypeStruct((gs, rows, width), BF)
+        body = reduce_gather_body
+        scratch = [VM((rows, width), F32), DMA((gs - 1,)), DMA((gs - 1,))] + scratch
     return pl.pallas_call(
-        functools.partial(reduce_body, zs, gs),
-        out_shape=jax.ShapeDtypeStruct((rows, width), F32),
+        functools.partial(body, zs, gs),
+        out_shape=shape,
         in_specs=[pl.BlockSpec(memory_space=pltpu.VMEM)],
         out_specs=pl.BlockSpec(memory_space=pltpu.VMEM),
-        scratch_shapes=[
-            VM((zs, gs, rows, width), BF),
-            VM((zs, gs, rows, width), BF),
-            VM((zs - 1, gs, rows, half), BF),
-            VM((gs - 1, zs, rows, half), BF),
-            VM((gs - 1, rows, half), BF),
-            VM((zs - 1, rows, half), BF),
-            VM((gs - 1, rows, half), BF),
-            VM((zs - 1, rows, half), BF),
-            DMA((zs,)), DMA((zs,)),
-            DMA((zs - 1,)), DMA((zs - 1,)),
-            DMA((gs - 1, zs)), DMA((gs - 1, zs)),
-            DMA((gs - 1,)), DMA((gs - 1,)),
-            DMA((zs - 1,)), DMA((zs - 1,)),
-        ],
+        scratch_shapes=scratch,
         compiler_params=pltpu.CompilerParams(collective_id=number, has_side_effects=True),
     )(x)
 
@@ -189,8 +215,8 @@
 def gather_body(zs, gs, y, out, cs, cr, a1s, a1r, b1s, b1r, a2s, a2r, b2s, b2r, ls):
     g, z, core = position(zs, gs)
     width = y.shape[-1]
-    half = width // 2
-    left, right = pl.ds(0, half), pl.ds(half, half)
+    half = cut_of(width)
+    left, right = pl.ds(0, half), pl.ds(half, width - half)
     greet(zs, gs, g, z, core)
     twin = (g, 2 * z + 1 - core)
     own = pltpu.make_async_copy(y, out.at[z, core, g], ls)
@@ -272,7 +298,7 @@
     tokens_all = key_tokens.shape[0] * devices
     weights = (w_gate, w_up, w_down)
     rows = 3 * full_width // devices
-    direct = 3 * full_width % (8 * devices) == 0 and toks % 4 == 0 and full_width % 256 == 0
+    direct = 3 * full_width % (8 * devices) == 0 and toks % 4 == 0 and full_width % 384 == 0
     me = lax.axis_index("tok") * gs + lax.axis_index("grp")
 
     def reduce_units(x, number):
@@ -309,8 +335,12 @@
     plain = (dot(queries.T, d_hgate), dot(queries.T, d_hup), dot(active.T, out_grad))
     combined = jnp.stack(tuple((left + right for left, right in zip(plain, second[:3]))))
     combined = combined.reshape(3, toks, full_width // toks, full_width).transpose(1, 0, 2, 3)
-    summed = reduce_units(combined, 4) * (1.0 / tokens_all)
-    summed = lax.all_gather(summed.astype(BF), "grp").astype(F32)
+    if direct:
+        units = combined.astype(BF).reshape(zs, 2, gs, rows, full_width)
+        summed = reduce_all(units, 4, True)
+    else:
+        summed = lax.all_gather(reduce_units(combined, 4).astype(BF), "grp")
+    summed = summed.astype(F32) * (1.0 / tokens_all)
     summed = summed.reshape(3, full_width // toks, full_width)
     return (d_queries, second[3], second[4], summed[0], summed[1], summed[2])
 

time: 247 us -> 220 us (0.89)
  Pallas kernels: 170 us -> 153 us
  blocking collectives: 9.15 us -> 0 us
    pallas_call x3, Pallas kernels: 109 us -> 94.5 us  [reduce_all(): pl.pallas_call(functools.partial(body, zs, gs), out_shape=shape, in_specs...]
    all_gather x1 -> x0, blocking collectives: 9.15 us -> none  [on_device(): summed = lax.all_gather(summed.astype(BF), 'grp').astype(F32)]
    pallas_call x2, Pallas kernels: 60.6 us -> 58.1 us  [gather_all(): pl.pallas_call(functools.partial(gather_body, zs, gs), out_shape=jax.Shap...]
where the time goes in v2:
time: 220 us
  Pallas kernels  153 us (70%)
  matrix products  29.3 us (13%)
  local copies, waits for them, and re-layouts  23.9 us (11%)
  other arithmetic  12.6 us (6%)
    pallas_call x3, Pallas kernels, reduce_all(): pl.pallas_call(functools.partial(body, zs, gs), out_shape=shape, in_specs...  94.5 us
    pallas_call x2, Pallas kernels, gather_all(): pl.pallas_call(functools.partial(gather_body, zs, gs), out_shape=jax.Shap...  58.1 us
    dot_general x21, matrix products, matmul(): jnp.dot(left.astype(BF), right.astype(BF), preferred_element_type=F32)  21.4 us
    unnamed x73, local copies, waits for them, and re-layouts  14.7 us
    add x2, local copies, waits for them, and re-layouts, on_device(): left + right  4.75 us

profile of v2, /device:TPU:0, one launch (start us, length us, event | category | flops | bytes accessed | tf_op | source)
XLA Modules:
  0.0 219.6 jit_solution(15518657850657529307)
XLA Ops:
  0.6 0.0 copy-start
  0.7 1.2 convert_element_type.174
  1.8 2.0 fusion.29
  3.9 0.3 multiply_convert_fusion.3
  4.2 1.6 copy-done.12
  5.8 0.1 convert_element_type.178
  6.0 0.3 fusion.5
  6.3 1.3 fusion.42
  7.7 0.5 fusion
  8.1 0.2 copy-done.21
  8.3 0.5 fusion.1
  8.8 0.5 fusion.2
  9.3 2.1 pad_maximum_fusion
  11.5 30.0 %shard_map.118 = f32[72,768]{1,0:T(8,128)} custom-call(bf16[4,2,4,72,768]{4,3,2,1,0:T(8,128)(2,1)} %bitcast.158), custom_call_target="tpu_custom_call" | custom-call | tf_op jit(solution)/shard_map/pallas_call | solution.py:205
  41.5 1.1 multiply_reduce_fusion.1
  42.5 3.1 %copy.29 = f32[768,768]{0,1:T(8,128)} copy(f32[768,768]{1,0:T(8,128)} %param.13) | data formatting | bytes 4718592 | tf_op args[6]
  45.6 3.1 %copy.27 = f32[768,768]{0,1:T(8,128)} copy(f32[768,768]{1,0:T(8,128)} %param.11) | data formatting | bytes 4718592 | tf_op args[4]
  48.7 2.0 copy.28
  50.7 1.7 fusion.48.y
  52.4 29.4 %shard_map.119 = bf16[4,2,4,72,768]{4,3,2,1,0:T(8,128)(2,1)} custom-call(bf16[72,768]{1,0:T(8,128)(2,1)} %fusion.48.y), custom_call_target="tpu_custom_call" | custom-call | tf_op jit(solution)/shard_map/pallas_call | solution.py:277
  81.9 2.0 convolution_bitcast_fusion.1
  83.8 1.8 convolution_bitcast_fusion.2
  85.6 0.4 multiply_convert_fusion.1
  86.1 0.3 fusion.24
  86.4 1.0 fusion.6
  87.4 0.5 fusion.49
  87.9 1.5 copy.33
  89.5 1.5 fusion.56
  91.0 0.5 fusion.55
  91.5 0.2 convert_bitcast_fusion.1
  91.7 0.7 copy-done.4
  92.4 0.7 copy-done.2
  93.2 0.5 copy-done.14
  93.6 1.9 pad_maximum_fusion.1
  95.6 29.1 %shard_map.120 = f32[72,768]{1,0:T(8,128)} custom-call(bf16[4,2,4,72,768]{4,3,2,1,0:T(8,128)(2,1)} %bitcast.159), custom_call_target="tpu_custom_call" | custom-call | tf_op jit(solution)/shard_map/pallas_call | solution.py:205
  124.6 1.1 multiply_reduce_fusion
  125.7 1.7 subtract_convert_fusion.y
  127.4 28.6 %shard_map.121 = bf16[4,2,4,72,768]{4,3,2,1,0:T(8,128)(2,1)} custom-call(bf16[72,768]{1,0:T(8,128)(2,1)} %subtract_convert_fusion.y), custom_call_target="tpu_custom_call" | custom-call | tf_op jit(solution)/shard_map/pallas_call | solution.py:277
  156.1 1.8 fusion.23
  157.9 2.4 %fusion.22 = f32[128,768]{1,0:T(8,128)} fusion(f32[128,768]{1,0:T(8,128)S(1)} %fusion.23, bf16[768,128]{0,1:T(8,128)(2,1)S(1)} %copy-done.20, bf16[3,768,768]{2,1,0:T(8,128)(2,1)} %bitcast.153), kind=kOutput, calls=%fused_computation.61 | convolution fusion | flops 151289856 | bytes 2162688 | tf_op jit(solution)/shard_map/transpose(jvp())/dot_general | solution.py:18
  160.3 0.5 fusion.20
  160.9 0.5 fusion.17
  161.4 0.3 fusion.18
  161.8 0.6 multiply_add_fusion.1
  162.4 0.7 copy-done.10
  163.0 1.1 fusion.54
  164.1 0.8 fusion.35
  165.0 0.9 copy-done.5
  165.9 1.6 fusion.4
  167.4 1.5 fusion.3
  168.9 2.4 %copy.37 = bf16[768,768]{1,0:T(8,128)(2,1)} copy(bf16[768,768]{0,1:T(8,128)(2,1)} %fusion.3) | data formatting | bytes 2359296 | tf_op jit(solution)/shard_map/add | solution.py:336
  171.3 2.4 %copy.39 = bf16[768,768]{1,0:T(8,128)(2,1)} copy(bf16[768,768]{0,1:T(8,128)(2,1)} %fusion.4) | data formatting | bytes 2359296 | tf_op jit(solution)/shard_map/add | solution.py:336
  173.7 2.5 %fusion.10 = f32[128,768]{1,0:T(8,128)S(1)} fusion(f32[128,768]{1,0:T(8,128)} %fusion.22, bf16[128,768]{1,0:T(8,128)(2,1)} %copy-done.26, f32[768,768]{1,0:T(8,128)} %param.12), kind=kOutput, calls=%fused_computation.42 | convolution fusion | flops 151781376 | bytes 3342336 | tf_op jit(solution)/shard_map/transpose(jvp())/dot_general | solution.py:18
  176.2 0.1 copy-done.7
  176.2 1.3 fusion.8
  177.5 0.5 fusion.57
  178.1 0.5 add_convert_fusion
  178.6 0.7 copy-done.15
  179.3 0.4 copy-done.16
  179.7 0.4 maximum_bitcast_fusion
  180.1 2.0 copy.40
  182.1 35.5 %shard_map.122 = bf16[4,72,768]{2,1,0:T(8,128)(2,1)} custom-call(bf16[4,2,4,72,768]{4,3,2,1,0:T(8,128)(2,1)} %bitcast.160), custom_call_target="tpu_custom_call" | custom-call | tf_op jit(solution)/shard_map/pallas_call | solution.py:205
  217.6 1.1 convert_multiply_fusion
  218.7 0.9 slice_bitcast_fusion.17
  (60 shorter events, 0.1 us)
Async XLA Ops:
  0.6 81.2 %copy-start = (bf16[128,768]{1,0:T(8,128)(2,1)S(1)}, bf16[128,768]{1,0:T(8,128)(2,1)}, u32[]{:S(2)}) copy-start(bf16[128,768]{1,0:T(8,128)(2,1)} %param.7) | copy-start | bytes 589828
  0.6 3.2 %copy-start.6 = (f32[768,768]{1,0:T(8,128)S(1)}, f32[768,768]{1,0:T(8,128)}, u32[]{:S(2)}) copy-start(f32[768,768]{1,0:T(8,128)} %param.12) | copy-start | bytes 7077892
  3.8 2.4 %copy-start.17 = (f32[128,768]{1,0:T(8,128)}, f32[128,768]{1,0:T(8,128)S(1)}, u32[]{:S(2)}) copy-start(f32[128,768]{1,0:T(8,128)S(1)} %fusion.29) | copy-start | bytes 1179652
  3.9 2.0 copy-start.12
  4.2 2.1 copy-start.30
  4.2 1.7 copy-start.32
  5.9 1.7 copy-start.9
  7.6 0.7 copy-start.21
  7.6 1.7 copy-start.19
  48.7 2.0 copy-start.13
  81.8 3.8 %copy-start.11 = (bf16[4,2,4,72,768]{4,3,2,1,0:T(8,128)(2,1)S(1)}, bf16[4,2,4,72,768]{4,3,2,1,0:T(8,128)(2,1)}, u32[]{:S(2)}) copy-start(bf16[4,2,4,72,768]{4,3,2,1,0:T(8,128)(2,1)} %shard_map.119) | copy-start | bytes 10616836
  81.8 3.8 %copy-start.33 = (bf16[128,768]{1,0:T(8,128)(2,1)S(1)}, bf16[128,768]{1,0:T(8,128)(2,1)}, u32[]{:S(2)}) copy-start(bf16[128,768]{1,0:T(8,128)(2,1)} %param.10) | copy-start | bytes 589828
  86.0 1.4 copy-start.27
  86.0 1.4 copy-start.29
  89.5 1.5 copy-start.28
  91.0 1.5 copy-start.4
  91.5 1.7 copy-start.2
  91.5 2.1 copy-start.14
  127.4 30.5 %copy-start.20 = (bf16[768,128]{0,1:T(8,128)(2,1)S(1)}, bf16[768,128]{0,1:T(8,128)(2,1)}, u32[]{:S(2)}) copy-start(bf16[768,128]{0,1:T(8,128)(2,1)} %copy-done.19) | copy-start | bytes 589828
  156.0 4.3 %copy-start.8 = (bf16[4,2,4,72,768]{4,3,2,1,0:T(8,128)(2,1)S(1)}, bf16[4,2,4,72,768]{4,3,2,1,0:T(8,128)(2,1)}, u32[]{:S(2)}) copy-start(bf16[4,2,4,72,768]{4,3,2,1,0:T(8,128)(2,1)} %shard_map.121) | copy-start | bytes 10616836
  160.3 1.4 copy-start.18
  160.3 1.4 copy-start.31
  161.8 1.3 copy-start.10
  161.8 2.3 %copy-start.34 = (f32[128,768]{1,0:T(8,128)S(1)}, f32[128,768]{1,0:T(8,128)}, u32[]{:S(2)}) copy-start(f32[128,768]{1,0:T(8,128)} %get-tuple-element.19) | copy-start | bytes 1179652
  164.1 0.8 copy-start.22
  164.1 1.7 copy-start.5
  164.9 2.5 %copy-start.26 = (bf16[128,768]{1,0:T(8,128)(2,1)}, bf16[128,768]{1,0:T(8,128)(2,1)S(1)}, u32[]{:S(2)}) copy-start(bf16[128,768]{1,0:T(8,128)(2,1)S(1)} %get-tuple-element.7) | copy-start | bytes 589828
  164.9 2.5 %copy-start.24 = (bf16[128,768]{1,0:T(8,128)(2,1)}, bf16[128,768]{1,0:T(8,128)(2,1)S(1)}, u32[]{:S(2)}) copy-start(bf16[128,768]{1,0:T(8,128)(2,1)S(1)} %get-tuple-element.6) | copy-start | bytes 589828
  165.0 2.5 %copy-start.3 = (f32[768,768]{1,0:T(8,128)S(1)}, f32[768,768]{1,0:T(8,128)}, u32[]{:S(2)}) copy-start(f32[768,768]{1,0:T(8,128)} %copy-done.2) | copy-start | bytes 7077892
  173.7 2.6 %copy-start.7 = (f32[768,768]{1,0:T(8,128)S(1)}, f32[768,768]{1,0:T(8,128)}, u32[]{:S(2)}) copy-start(f32[768,768]{1,0:T(8,128)} %param.11) | copy-start | bytes 7077892
  173.7 2.6 %copy-start.25 = (bf16[128,768]{1,0:T(8,128)(2,1)S(1)}, bf16[128,768]{1,0:T(8,128)(2,1)}, u32[]{:S(2)}) copy-start(bf16[128,768]{1,0:T(8,128)(2,1)} %copy-done.24) | copy-start | bytes 589828
  176.2 1.3 copy-start.23
  178.0 1.3 copy-start.15
  178.0 1.6 copy-start.16
  182.1 37.5 %copy-start.1 = (bf16[128,768]{1,0:T(8,128)(2,1)S(1)}, bf16[128,768]{1,0:T(8,128)(2,1)}, u32[]{:S(2)}) copy-start(bf16[128,768]{1,0:T(8,128)(2,1)} %param.7) | copy-start | bytes 589828
